TPU v7x, 256 devices: a whole 4x4x8 slice. The times are simulated.
256 devices in a mesh: dp: 32 (over y, z), cent: 8 (over x, core).
Axes of the slice: x: 4, y: 4, z: 8, core: 2. Of those that a mesh axis runs over, the one named last changes fastest.
Arguments:
- embeddings: bfloat16 [16384, 768], P('dp'), may hold values from -400 to 400, as said below
- centroids: bfloat16 [16384, 768], P('cent'), may hold values from -400 to 400, as said below
Outputs:
- new_centroids: float32 [16384, 768], P(('cent', 'dp'))
Inputs may be any that keep to these rules, and one draw needn't show every extreme that they name: `embeddings`: finite real values. `centroids`: finite real values.
All inputs are finite; a program needn't handle non-finite values.
Results may differ from a plain program's by a relative error of at most 0.0038.
Values sent between devices are 32-bit elements; how exact they have to be, the bound alone decides.
A program may use at most 64 MiB of HBM per device.

v0:
```python
import jax
import jax.numpy as jnp
from jax import lax
from jax.sharding import PartitionSpec as P

FEATURE_DIM = 768
ROUNDS = 2
entropy_regularizer = 0.05


def normalize(values):
    wide = values.astype(jnp.float32)
    meansq = jnp.mean(wide * wide, axis=-1, keepdims=True)
    return (wide * lax.rsqrt(meansq + 1e-06)).astype(jnp.bfloat16)


def row_update(boltzmann_affinity, column_factor):
    partial_rows = jnp.dot(boltzmann_affinity, column_factor, precision=lax.Precision.HIGHEST)
    totals = lax.psum(partial_rows, "cent")
    return 1.0 / totals


def shards(embeddings, centroids):
    normed = normalize(embeddings)
    cent_normed = normalize(centroids)
    cosine_matches = lax.dot_general(
        normed, cent_normed, (((1,), (1,)), ((), ())), preferred_element_type=jnp.float32
    )
    boltzmann_affinity = jnp.exp(cosine_matches * (1.0 / (FEATURE_DIM * entropy_regularizer)))
    local_cents = centroids.shape[0]
    row_count = embeddings.shape[0] * lax.axis_size("dp")
    cent_count = local_cents * lax.axis_size("cent")
    balance_ratio = row_count / cent_count
    column_factor = jnp.ones((local_cents,), jnp.float32)
    for sweep in range(ROUNDS):
        row_weight = row_update(boltzmann_affinity, column_factor)
        partial_cols = jnp.dot(row_weight, boltzmann_affinity, precision=lax.Precision.HIGHEST)
        column_factor = balance_ratio / lax.psum(partial_cols, "dp")
    row_weight = row_update(boltzmann_affinity, column_factor)
    transport = (row_weight[:, None] * boltzmann_affinity * column_factor[None, :]).astype(
        jnp.bfloat16
    )
    col_mass = jnp.sum(transport, axis=0, dtype=jnp.float32)
    own_rows = local_cents // lax.axis_size("dp")
    holder_position = lax.axis_index("dp")
    weighted = lax.dot_general(
        transport, normed, (((0,), (0,)), ((), ())), preferred_element_type=jnp.float32
    )
    weighted, col_mass = lax.psum((weighted, col_mass), "dp")
    weighted = lax.dynamic_slice_in_dim(weighted, holder_position * own_rows, own_rows, 0)
    col_mass = lax.dynamic_slice_in_dim(col_mass, holder_position * own_rows, own_rows, 0)
    return weighted / col_mass[:, None]


def solution(mesh):
    in_specs = (P("dp", None), P("cent", None))
    out_specs = P(("cent", "dp"), None)
    return jax.shard_map(shards, mesh=mesh, in_specs=in_specs, out_specs=out_specs, check_vma=False)
```

profile of v0, /device:TPU:1, one launch (start us, length us, event | category | flops | bytes accessed | tf_op | source)
XLA Modules:
  0.0 423.9 jit_solution(16495555627973379805)
XLA Ops:
  6.5 0.0 all-reduce.2.cloned.1.call-start
  6.5 1.4 fusion.4
  7.9 2.6 fusion
  10.5 4.1 multiply_exponential_fusion
  14.6 0.0 copy-start
  14.6 1.9 copy-done
  16.6 3.6 fusion.9
  20.2 15.0 %psum.49 = f32[512]{0:T(512)S(1)} all-reduce(f32[512]{0:T(512)S(1)} %bitcast.25), channel_id=1, replica_groups=mesh['dp'=32,'cent'=8] {'cent'}, use_global_device_ids=true, to_apply=%region_2.0 | all-reduce | flops 512 | bytes 4096 | tf_op jit(solution)/shard_map/psum | solution.py:19
  35.2 4.3 %fusion.12 = f32[1,2048]{1,0:T(1,128)S(1)} fusion(f32[512,1]{0,1:T(1,128)S(1)} %bitcast.22, f32[512,2048]{1,0:T(8,128)} %copy-done), kind=kOutput, calls=%fused_computation.24 | convolution fusion | flops 12582912 | bytes 4204544 | tf_op jit(solution)/shard_map/dot_general | solution.py:37
  39.4 63.4 %psum.50 = f32[2048]{0:T(1024)S(1)} all-reduce(f32[2048]{0:T(1024)S(1)} %bitcast.19), channel_id=1, replica_groups=mesh['dp'=32,'cent'=8] {'dp'}, use_global_device_ids=true, to_apply=%region_3.0 | all-reduce | flops 2048 | bytes 16384 | tf_op jit(solution)/shard_map/psum | solution.py:38
  102.9 5.8 %fusion.13 = f32[1,512]{1,0:T(1,128)S(1)} fusion(f32[512,2048]{1,0:T(8,128)} %copy-done, f32[2048,1]{0,1:T(1,128)S(1)} %bitcast.20), kind=kOutput, calls=%fused_computation.25 | convolution fusion | flops 12582912 | bytes 4204544 | tf_op jit(solution)/shard_map/dot_general | solution.py:18
  108.6 28.6 %psum.51 = f32[512]{0:T(512)S(1)} all-reduce(f32[512]{0:T(512)S(1)} %bitcast.23), channel_id=1, replica_groups=mesh['dp'=32,'cent'=8] {'cent'}, use_global_device_ids=true, to_apply=%region_4.0 | all-reduce | flops 512 | bytes 4096 | tf_op jit(solution)/shard_map/psum | solution.py:19
  137.2 0.0 copy-start.1
  137.2 4.3 %fusion.14 = f32[1,2048]{1,0:T(1,128)S(1)} fusion(f32[512,1]{0,1:T(1,128)S(1)} %bitcast.24, f32[512,2048]{1,0:T(8,128)} %copy-done), kind=kOutput, calls=%fused_computation.26 | convolution fusion | flops 12582912 | bytes 4204544 | tf_op jit(solution)/shard_map/dot_general | solution.py:37
  141.6 57.2 %psum.52 = f32[2048]{0:T(1024)S(1)} all-reduce(f32[2048]{0:T(1024)S(1)} %bitcast.21), channel_id=1, replica_groups=mesh['dp'=32,'cent'=8] {'dp'}, use_global_device_ids=true, to_apply=%region_5.0 | all-reduce | flops 2048 | bytes 16384 | tf_op jit(solution)/shard_map/psum | solution.py:38
  198.8 5.8 %fusion.15 = f32[1,512]{1,0:T(1,128)S(1)} fusion(f32[512,2048]{1,0:T(8,128)} %copy-done, f32[2048,1]{0,1:T(1,128)S(1)} %bitcast.18), kind=kOutput, calls=%fused_computation.27 | convolution fusion | flops 12582912 | bytes 4204544 | tf_op jit(solution)/shard_map/dot_general | solution.py:18
  204.6 25.8 %psum.53 = f32[512]{0:T(512)S(1)} all-reduce(f32[512]{0:T(512)S(1)} %bitcast.26), channel_id=1, replica_groups=mesh['dp'=32,'cent'=8] {'cent'}, use_global_device_ids=true, to_apply=%region_6.0 | all-reduce | flops 512 | bytes 4096 | tf_op jit(solution)/shard_map/psum | solution.py:19
  230.4 0.0 copy-done.1
  230.4 6.8 %fusion.6 = f32[2048,768]{1,0:T(8,128)} fusion(bf16[512,768]{1,0:T(8,128)(2,1)S(1)} %copy-done.1, f32[512]{0:T(512)S(1)} %add_rsqrt_fusion.1, f32[512,2048]{1,0:T(8,128)} %copy-done, f32[2048]{0:T(1024)S(1)} %broadcast_divide_fusion.1, f32[512]{0:T(512)S(1)} %broadcast_divide_fusion.2), kind=kOutput, calls=%fused_computation.12 | convolution fusion | flops 1614938112 | bytes 11284480 | tf_op jit(solution)/shard_map/dot_general | solution.py:46
  237.3 0.0 all-reduce.2.cloned.1.call-update
  237.3 2.7 convert_reduce_fusion
  240.0 62.2 %psum.55 = f32[2048]{0:T(1024)S(1)} all-reduce(f32[2048]{0:T(1024)S(1)} %convert_reduce_fusion), channel_id=1, replica_groups=mesh['dp'=32,'cent'=8] {'dp'}, use_global_device_ids=true, to_apply=%region_9.0 | all-reduce | flops 2048 | bytes 16384 | tf_op jit(solution)/shard_map/psum | solution.py:49
  302.2 0.1 dynamic_slice.7
  302.3 113.1 %all-reduce.2.cloned.1.call-done = f32[2048,768]{1,0:T(8,128)} async-done(((f32[2048,768]{1,0:T(8,128)}), f32[2048,768]{1,0:T(8,128)}) %all-reduce.2.cloned.1.call-update) | async-done | bytes 6291472 | tf_op jit(solution)/shard_map/psum | solution.py:49
  415.3 1.7 dynamic-slice_divide_fusion
  (7 shorter events, 0.0 us)
Async XLA Ops:
  6.5 408.8 %all-reduce.2.cloned.1.call-start = ((), (), s32[]{:S(2)}) async-start(), calls=%async_computation | async-start | bytes 12582912 | tf_op jit(solution)/shard_map/psum | solution.py:49
  14.6 2.0 copy-start
  137.2 93.2 %copy-start.1 = (bf16[512,768]{1,0:T(8,128)(2,1)S(1)}, bf16[512,768]{1,0:T(8,128)(2,1)}, u32[]{:S(2)}) copy-start(bf16[512,768]{1,0:T(8,128)(2,1)} %param.2) | copy-start | bytes 2359300
Sparse Core Ops, SparseCore 0:
  237.4 177.8 all-reduce.1
where the time goes:
time: 424 us
  blocking collectives  252 us (59%)
  waiting for transfers between devices  113 us (27%)
  matrix products  34.7 us (8%)
  between operations  13.5 us (3%)
  other arithmetic  8.35 us (2%)
    psum x2, blocking collectives, shards(): column_factor = balance_ratio / lax.psum(partial_cols, 'dp')  121 us
    psum x1, waiting for transfers between devices, shards(): weighted, col_mass = lax.psum((weighted, col_mass), 'dp')  113 us
    psum x3, blocking collectives, row_update(): totals = lax.psum(partial_rows, 'cent')  69.4 us
    psum x1, blocking collectives, shards(): weighted, col_mass = lax.psum((weighted, col_mass), 'dp')  62.2 us
    dot_general x3, matrix products, row_update(): jnp.dot(boltzmann_affinity, column_factor, precision=lax.Precision.HIGHEST)  15.1 us
    dot_general x2, matrix products, shards(): jnp.dot(row_weight, boltzmann_affinity, precision=lax.Precision.HIGHEST)  8.61 us
  transfers between devices with their start and end apart: 1, of which 1 were waited for; matrix products, arithmetic and copies ran while one was open for 1% of the time, Pallas kernels for 0%

commit v1 on v0

--- a/solution.py
+++ b/solution.py
@@ -16,7 +16,11 @@
 
 def row_update(boltzmann_affinity, column_factor):
     partial_rows = jnp.dot(boltzmann_affinity, column_factor, precision=lax.Precision.HIGHEST)
-    totals = lax.psum(partial_rows, "cent")
+    size = lax.axis_size("cent")
+    totals, hop = (partial_rows, 1)
+    while hop < size:
+        totals = totals + lax.ppermute(totals, "cent", [(i, i ^ hop) for i in range(size)])
+        hop = 2 * hop
     return 1.0 / totals
 
 

time: 424 us -> 409 us (0.965)
  blocking collectives: 252 us -> 181 us
  starting transfers between devices: 0.01 us -> 45.4 us
  waiting for transfers between devices: 113 us -> 131 us
  matrix products: 34.7 us -> 28.4 us
    psum x3 -> x0, blocking collectives: 69.4 us -> none  [row_update(): totals = lax.psum(partial_rows, 'cent')]
    ppermute x0 -> x9, starting transfers between devices: none -> 45.4 us  [row_update(): lax.ppermute(totals, 'cent', [(i, i ^ hop) for i in range(size)])]
    ppermute x0 -> x9, waiting for transfers between devices: none -> 12.7 us  [row_update(): lax.ppermute(totals, 'cent', [(i, i ^ hop) for i in range(size)])]
    psum x1, waiting for transfers between devices: 113 us -> 119 us  [shards(): weighted, col_mass = lax.psum((weighted, col_mass), 'dp')]
    dot_general x2, matrix products: 8.61 us -> 4.15 us  [shards(): jnp.dot(row_weight, boltzmann_affinity, precision=lax.Precision.HIGHEST)]
  transfers between devices with their start and end apart: 1 -> 10, of which waited for: 1 -> 10; matrix products, arithmetic and copies ran while one was open for 1% -> 1% of each run, Pallas kernels for 0% -> 0%
where the time goes in v1:
time: 409 us; the launch traced here: 408 us
  blocking collectives  181 us (44%)
  waiting for transfers between devices  131 us (32%)
  starting transfers between devices  45.4 us (11%)
  matrix products  28.4 us (7%)
  between operations  13.5 us (3%)
  other arithmetic  8.37 us (2%)
    psum x2, blocking collectives, shards(): column_factor = balance_ratio / lax.psum(partial_cols, 'dp')  120 us
    psum x1, waiting for transfers between devices, shards(): weighted, col_mass = lax.psum((weighted, col_mass), 'dp')  119 us
    psum x1, blocking collectives, shards(): weighted, col_mass = lax.psum((weighted, col_mass), 'dp')  61 us
    ppermute x9, starting transfers between devices, row_update(): lax.ppermute(totals, 'cent', [(i, i ^ hop) for i in range(size)])  45.4 us
    dot_general x3, matrix products, row_update(): jnp.dot(boltzmann_affinity, column_factor, precision=lax.Precision.HIGHEST)  15.4 us
    ppermute x9, waiting for transfers between devices, row_update(): lax.ppermute(totals, 'cent', [(i, i ^ hop) for i in range(size)])  12.7 us
  transfers between devices with their start and end apart: 10, of which 10 were waited for; matrix products, arithmetic and copies ran while one was open for 1% of the time, Pallas kernels for 0%

profile of v1, /device:TPU:1, one launch (start us, length us, event | category | flops | bytes accessed | tf_op | source)
XLA Modules:
  0.0 408.3 jit_solution(7892061383444774427)
XLA Ops:
  6.5 0.0 all-reduce.2.cloned.1.call-start
  6.5 1.4 fusion.4
  7.9 2.6 fusion
  10.5 4.1 %multiply_exponential_fusion = f32[512,2048]{1,0:T(8,128)S(1)} fusion(bf16[2048,768]{1,0:T(8,128)(2,1)} %param.3, f32[2048]{0:T(1024)S(1)} %add_rsqrt_fusion, bf16[512,768]{1,0:T(8,128)(2,1)} %param.2, f32[512]{0:T(512)S(1)} %add_rsqrt_fusion.1), kind=kOutput, calls=%fused_computation.6 | convolution fusion | flops 1617559552 | bytes 8136704 | tf_op jit(solution)/shard_map/dot_general | solution.py:30
  14.6 0.0 copy-start
  14.6 3.6 fusion.9
  18.2 3.2 collective-permute-start
  21.5 0.8 collective-permute-done
  22.3 0.0 collective-permute-start.1
  22.3 2.4 collective-permute-done.1
  24.7 1.0 collective-permute-start.2
  25.8 2.9 collective-permute-done.2
  28.7 2.1 fusion.12
  30.8 0.0 copy-done
  30.8 63.4 %psum.28 = f32[2048]{0:T(1024)S(1)} all-reduce(f32[2048]{0:T(1024)S(1)} %bitcast.19), channel_id=1, replica_groups=mesh['dp'=32,'cent'=8] {'dp'}, use_global_device_ids=true, to_apply=%region_2.0 | all-reduce | flops 2048 | bytes 16384 | tf_op jit(solution)/shard_map/psum | solution.py:42
  94.1 0.0 copy-start.1
  94.1 5.9 %fusion.13 = f32[1,512]{1,0:T(1,128)S(1)} fusion(f32[512,2048]{1,0:T(8,128)} %copy-done, f32[2048,1]{0,1:T(1,128)S(1)} %bitcast.20), kind=kOutput, calls=%fused_computation.25 | convolution fusion | flops 12582912 | bytes 4204544 | tf_op jit(solution)/shard_map/dot_general | solution.py:18
  100.1 16.7 %collective-permute-start.3 = (f32[512]{0:T(512)S(1)}, f32[512]{0:T(512)S(1)}, u32[]{:S(2)}, u32[]{:S(2)}) collective-permute-start(f32[512]{0:T(512)S(1)} %bitcast.22), channel_id=1, source_target_pairs={{0,1},{1,0},{2,3},{3,2},{4,5},{5,4},{6,7},{7,6},{8,9},{9,8},{10,11... | collective-permute-start | bytes 6152 | tf_op jit(solution)/shard_map/ppermute | solution.py:22
  116.8 0.8 collective-permute-done.3
  117.6 1.2 collective-permute-start.4
  118.8 1.2 collective-permute-done.4
  120.0 2.7 collective-permute-start.5
  122.8 1.2 collective-permute-done.5
  124.0 0.0 copy-done.1
  124.0 0.0 copy-start.3
  124.0 2.1 fusion.14
  126.1 56.7 %psum.29 = f32[2048]{0:T(1024)S(1)} all-reduce(f32[2048]{0:T(1024)S(1)} %bitcast.21), channel_id=1, replica_groups=mesh['dp'=32,'cent'=8] {'dp'}, use_global_device_ids=true, to_apply=%region_3.0 | all-reduce | flops 2048 | bytes 16384 | tf_op jit(solution)/shard_map/psum | solution.py:42
  182.8 0.0 copy-start.2
  182.8 5.9 %fusion.15 = f32[1,512]{1,0:T(1,128)S(1)} fusion(f32[512,2048]{1,0:T(8,128)} %copy-done, f32[2048,1]{0,1:T(1,128)S(1)} %bitcast.18), kind=kOutput, calls=%fused_computation.27 | convolution fusion | flops 12582912 | bytes 4204544 | tf_op jit(solution)/shard_map/dot_general | solution.py:18
  188.7 16.6 %collective-permute-start.6 = (f32[512]{0:T(512)S(1)}, f32[512]{0:T(512)S(1)}, u32[]{:S(2)}, u32[]{:S(2)}) collective-permute-start(f32[512]{0:T(512)S(1)} %bitcast.26), channel_id=1, source_target_pairs={{0,1},{1,0},{2,3},{3,2},{4,5},{5,4},{6,7},{7,6},{8,9},{9,8},{10,11... | collective-permute-start | bytes 6152 | tf_op jit(solution)/shard_map/ppermute | solution.py:22
  205.3 0.8 collective-permute-done.6
  206.1 1.2 collective-permute-start.7
  207.3 1.2 collective-permute-done.7
  208.6 2.7 collective-permute-start.8
  211.3 1.2 collective-permute-done.8
  212.5 0.0 copy-done.3
  212.5 0.0 copy-done.2
  212.5 4.7 %fusion.6 = f32[2048,768]{1,0:T(8,128)} fusion(bf16[512,768]{1,0:T(8,128)(2,1)S(1)} %copy-done.3, f32[512]{0:T(512)S(1)} %add_rsqrt_fusion.1, f32[512,2048]{1,0:T(8,128)S(1)} %copy-done.2, f32[2048]{0:T(1024)S(1)} %broadcast_divide_fusion.1, f32[512]{0:T(512)S(1)} %add_divide_fusion), kind=kOutput, calls=%fused_computation.12 | convolution fusion | flops 1614938112 | bytes 11284480 | tf_op jit(solution)/shard_map/dot_general | solution.py:50
  217.2 0.0 all-reduce.2.cloned.1.call-update
  217.3 2.7 convert_reduce_fusion
  220.0 61.0 %psum.31 = f32[2048]{0:T(1024)S(1)} all-reduce(f32[2048]{0:T(1024)S(1)} %convert_reduce_fusion), channel_id=1, replica_groups=mesh['dp'=32,'cent'=8] {'dp'}, use_global_device_ids=true, to_apply=%region_6.0 | all-reduce | flops 2048 | bytes 16384 | tf_op jit(solution)/shard_map/psum | solution.py:53
  281.0 0.1 dynamic_slice.7
  281.1 118.6 %all-reduce.2.cloned.1.call-done = f32[2048,768]{1,0:T(8,128)} async-done(((f32[2048,768]{1,0:T(8,128)}), f32[2048,768]{1,0:T(8,128)}) %all-reduce.2.cloned.1.call-update) | async-done | bytes 6291472 | tf_op jit(solution)/shard_map/psum | solution.py:53
  399.7 1.7 dynamic-slice_divide_fusion
  (13 shorter events, 0.1 us)
Async XLA Ops:
  6.5 393.2 %all-reduce.2.cloned.1.call-start = ((), (), s32[]{:S(2)}) async-start(), calls=%async_computation | async-start | bytes 12582912 | tf_op jit(solution)/shard_map/psum | solution.py:53
  14.6 16.1 %copy-start = (f32[512,2048]{1,0:T(8,128)}, f32[512,2048]{1,0:T(8,128)S(1)}, u32[]{:S(2)}) copy-start(f32[512,2048]{1,0:T(8,128)S(1)} %multiply_exponential_fusion) | copy-start | bytes 12582916
  18.2 4.0 collective-permute-start
  22.3 2.4 collective-permute-start.1
  24.7 3.9 collective-permute-start.2
  94.1 29.9 %copy-start.1 = (f32[512,2048]{1,0:T(8,128)S(1)}, f32[512,2048]{1,0:T(8,128)}, u32[]{:S(2)}) copy-start(f32[512,2048]{1,0:T(8,128)} %copy-done) | copy-start | bytes 12582916
  100.1 17.5 %collective-permute-start.3 = (f32[512]{0:T(512)S(1)}, f32[512]{0:T(512)S(1)}, u32[]{:S(2)}, u32[]{:S(2)}) collective-permute-start(f32[512]{0:T(512)S(1)} %bitcast.22), channel_id=1, source_target_pairs={{0,1},{1,0},{2,3},{3,2},{4,5},{5,4},{6,7},{7,6},{8,9},{9,8},{10,11... | collective-permute-start | bytes 6152 | tf_op jit(solution)/shard_map/ppermute | solution.py:22
  117.6 2.4 collective-permute-start.4
  120.0 3.9 collective-permute-start.5
  124.0 88.5 %copy-start.3 = (bf16[512,768]{1,0:T(8,128)(2,1)S(1)}, bf16[512,768]{1,0:T(8,128)(2,1)}, u32[]{:S(2)}) copy-start(bf16[512,768]{1,0:T(8,128)(2,1)} %param.2) | copy-start | bytes 2359300
  182.8 29.7 %copy-start.2 = (f32[512,2048]{1,0:T(8,128)S(1)}, f32[512,2048]{1,0:T(8,128)}, u32[]{:S(2)}) copy-start(f32[512,2048]{1,0:T(8,128)} %copy-done) | copy-start | bytes 12582916
  188.7 17.4 %collective-permute-start.6 = (f32[512]{0:T(512)S(1)}, f32[512]{0:T(512)S(1)}, u32[]{:S(2)}, u32[]{:S(2)}) collective-permute-start(f32[512]{0:T(512)S(1)} %bitcast.26), channel_id=1, source_target_pairs={{0,1},{1,0},{2,3},{3,2},{4,5},{5,4},{6,7},{7,6},{8,9},{9,8},{10,11... | collective-permute-start | bytes 6152 | tf_op jit(solution)/shard_map/ppermute | solution.py:22
  206.1 2.4 collective-permute-start.7
  208.6 3.9 collective-permute-start.8
Sparse Core Ops, SparseCore 0:
  217.4 182.2 all-reduce.1
